TPU v7x, 128 devices: a whole 4x4x4 slice. The times are simulated.
128 devices in a mesh: section: 2 (over core), dp: 16 (over y, x), mp: 4 (over z).
Axes of the slice: x: 4, y: 4, z: 4, core: 2. Of those that a mesh axis runs over, the one named last changes fastest.
Arguments:
- patches: bfloat16 [8192, 1280], P(('section', 'dp', 'mp')), may hold values from -6 to 6
- image_units: int32 [128, 3], P(('section', 'dp', 'mp')), may hold values from 1 to 8, 16 in all within a row
- v_gain: float32 [1280], replicated, may hold values from 0.5 to 1.5
- v_qkv: bfloat16 [1280, 3840], replicated, may hold values from -0.15625 to 0.15625
- v_out: bfloat16 [1280, 1280], replicated, may hold values from -0.15625 to 0.15625
- merge_gain: float32 [1280], replicated, may hold values from 0.5 to 1.5
- w_merge: bfloat16 [5120, 8192], P('dp', 'mp'), may hold values from -0.078125 to 0.078125
- routes: int32 [2048, 1], P(('section', 'dp', 'mp')), may hold values from 0 to 15; in each aligned block of 1024 rows (0 to 1023, 1024 to 2047, ...) at most 128 rows name the same one
- text: bfloat16 [4096, 8192], P(('section', 'dp'), 'mp'), may hold values from -6 to 6
- seq_lengths: int32 [32, 3], P(('section', 'dp')), may hold values from 1 to 64, 128 in all within a row
- lang_gain: float32 [2, 8192], P('section'), may hold values from 0.5 to 1.5
- w_qkv: bfloat16 [2, 8192, 5120], P('section', 'dp', 'mp'), may hold values from -0.0625 to 0.0625
- wo_t: bfloat16 [2, 8192, 4096], P('section', 'dp', 'mp'), may hold values from -0.09375 to 0.09375
- row_grads: bfloat16 [4096, 8192], P(('section', 'dp'), 'mp'), may hold values from -6 to 6
Outputs:
- final_hidden: bfloat16 [4096, 8192], P(('section', 'dp'), 'mp')
- merged_grads: bfloat16 [2048, 8192], P(('section', 'dp', 'mp'))
Inputs may be any that keep to these rules, and one draw needn't show every extreme that they name: `image_units`: each row sums to 16. `routes`: among the 1024 rows of one section index (aligned blocks), at most 128 name one group; in some section index one group is named by exactly 128. `seq_lengths`: each row sums to 128.
All inputs are finite; a program needn't handle non-finite values.
Results may differ from a plain program's by a relative error of at most 0.03.
Values may be sent and summed in bfloat16 or wider, within the bound.
A program may use at most 192 MiB of HBM per device.

v0:
```python
import math
import jax
import jax.numpy as jnp
from jax import lax
from jax.sharding import PartitionSpec as P

QH = 32
KVH = 4
HD = 128
VD = 1280
VH = 16
VHD = 80
MERGE = 4
EPSILON = 1e-06


def passed_along(value, axis, steps):
    count = lax.axis_size(axis)
    initial, last = (max(0, -steps), min(count, count - steps))
    return lax.ppermute(value, axis, [(source, source + steps) for source in range(initial, last)])


def broadcast(block, axis, owner):
    block = jnp.where(lax.axis_index(axis) == owner, block, jnp.zeros_like(block))
    return lax.psum(block, axis)


def layer_norm(values, norm_gain):
    values = values.astype(jnp.float32)
    centre = jnp.mean(values, axis=-1, keepdims=True)
    centred = values - centre
    variance = jnp.mean(centred * centred, axis=-1, keepdims=True)
    return centred * lax.rsqrt(variance + EPSILON) * norm_gain


def rms_norm(values, norm_gain):
    values = values.astype(jnp.float32)
    return (
        values * lax.rsqrt(jnp.mean(values * values, axis=-1, keepdims=True) + EPSILON) * norm_gain
    )


def segment_of(lengths, amount):
    boundary = jnp.cumsum(lengths.astype(jnp.int32))
    positions = jnp.arange(amount, dtype=jnp.int32)
    return jnp.sum((positions[:, None] >= boundary[None, :]).astype(jnp.int32), axis=1)


def vision_rows(patches, units, v_gain, v_qkv, v_out, merge_gain):
    amount = patches.shape[0]
    merged_count = amount // MERGE
    unit_image = segment_of(units, merged_count)
    image_ids = jnp.broadcast_to(unit_image[:, None], (merged_count, MERGE)).reshape(amount)
    v_normed = layer_norm(patches, v_gain).astype(jnp.bfloat16)
    projected = jnp.dot(v_normed, v_qkv, preferred_element_type=jnp.float32).astype(jnp.bfloat16)
    projected = projected.reshape(amount, 3, VH, VHD)
    scores = jnp.einsum(
        "qhd,khd->hqk", projected[:, 0], projected[:, 1], preferred_element_type=jnp.float32
    ) / math.sqrt(VHD)
    allowed = image_ids[:, None] == image_ids[None, :]
    scores = jnp.where(allowed[None], scores, -1e30)
    weights = jax.nn.softmax(scores, axis=-1).astype(jnp.bfloat16)
    attended = (
        jnp.einsum("hqk,khd->qhd", weights, projected[:, 2], preferred_element_type=jnp.float32)
        .astype(jnp.bfloat16)
        .reshape(amount, VD)
    )
    update = jnp.dot(attended, v_out, preferred_element_type=jnp.float32)
    v_hidden = (patches.astype(jnp.float32) + update).astype(jnp.bfloat16)
    merged = layer_norm(v_hidden, merge_gain).astype(jnp.bfloat16)
    return merged.reshape(merged_count, MERGE * VD)


def attend(projected, lengths):
    seq_rows = projected.shape[0]
    group_size = QH // KVH
    kv_here = projected.shape[1] // ((group_size + 2) * HD)
    heads_view = projected.reshape(seq_rows, kv_here, group_size + 2, HD)
    scores = jnp.einsum(
        "tkgd,skd->kgts",
        heads_view[:, :, :group_size],
        heads_view[:, :, group_size],
        preferred_element_type=jnp.float32,
    ) * (1.0 / math.sqrt(HD))
    seq_ids = segment_of(lengths, seq_rows)
    positions = jnp.arange(seq_rows, dtype=jnp.int32)
    allowed = (seq_ids[:, None] == seq_ids[None, :]) & (positions[:, None] >= positions[None, :])
    scores = jnp.where(allowed[None, None], scores, -1e30)
    weights = jax.nn.softmax(scores, axis=-1).astype(jnp.bfloat16)
    attended = jnp.einsum(
        "kgts,skd->tkgd",
        weights,
        heads_view[:, :, group_size + 1],
        preferred_element_type=jnp.float32,
    ).astype(jnp.bfloat16)
    return attended.reshape(seq_rows, kv_here * group_size * HD)


def shards(
    patches,
    image_units,
    v_gain,
    v_qkv,
    v_out,
    merge_gain,
    w_merge,
    routes,
    text,
    seq_lengths,
    lang_gain,
    w_qkv,
    wo_t,
    row_grads,
):
    merged = vision_rows(patches, image_units[0], v_gain, v_qkv, v_out, merge_gain)
    all_rows, all_routes = (
        lax.all_gather(merged, ("dp", "mp"), axis=0, tiled=True),
        lax.all_gather(routes, ("dp", "mp"), axis=0, tiled=True),
    )
    target = all_routes[:, 0]
    section_rows = target.shape[0]
    row_order = jnp.arange(section_rows, dtype=jnp.int32)
    matching = target[:, None] == target[None, :]
    position = jnp.sum(
        (matching & (row_order[:, None] > row_order[None, :])).astype(jnp.int32), axis=1
    )
    seq_rows = text.shape[0]
    slot_index = target * seq_rows + position
    group_here = lax.axis_index("dp")
    dp_count = lax.axis_size("dp")
    slice_width = w_merge.shape[0]
    row_slice = lax.dynamic_slice_in_dim(all_rows, group_here * slice_width, slice_width, 1)
    wanted = jnp.arange(seq_rows * lax.axis_size("dp"), dtype=jnp.int32)
    picker = (slot_index[None, :] == wanted[:, None]).astype(jnp.bfloat16)
    picked = jnp.dot(picker, row_slice, preferred_element_type=jnp.float32).astype(jnp.bfloat16)
    image_rows = lax.psum_scatter(
        jnp.dot(picked, w_merge, preferred_element_type=jnp.float32).astype(jnp.bfloat16),
        "dp",
        scatter_dimension=0,
        tiled=True,
    )
    present = jnp.sum((target == group_here).astype(jnp.int32))
    positions = jnp.arange(seq_rows, dtype=jnp.int32)
    entry_rows = jnp.where((positions < present)[:, None], image_rows, text)
    gathered = (
        lax.all_gather(w_qkv, "dp", axis=1, tiled=True),
        lax.all_gather(wo_t, "dp", axis=1, tiled=True),
    )
    qkv_weight = gathered[0][0]
    out_weight = gathered[1][0]
    norm_gain = lang_gain[0]
    sections = lax.axis_size("section")
    section_here = lax.axis_index("section")
    is_first = section_here == 0
    lengths_here = seq_lengths[0]
    entry_all, lengths_all = (
        lax.all_gather(entry_rows, "section", axis=0, tiled=True),
        lax.all_gather(seq_lengths, "section", axis=0, tiled=True),
    )
    carried = jnp.zeros_like(entry_rows)
    carried_lengths = lengths_here
    finished = []
    for section_step in range(2 * sections - 1):
        if section_step > 0:
            carried, carried_lengths = passed_along((carried, carried_lengths), "section", 1)
        if section_step < sections:
            incoming = entry_all[section_step * seq_rows : (section_step + 1) * seq_rows]
            incoming_lengths = lengths_all[section_step]
            carried = jnp.where(is_first, incoming, carried)
            carried_lengths = jnp.where(is_first, incoming_lengths, carried_lengths)
        features = lax.all_gather(carried, "mp", axis=1, tiled=True)
        normed = rms_norm(features, norm_gain).astype(jnp.bfloat16)
        projected = jnp.dot(normed, qkv_weight, preferred_element_type=jnp.float32)
        attended = attend(projected.astype(jnp.bfloat16), carried_lengths)
        partial_value = lax.dot_general(
            attended, out_weight, (((1,), (1,)), ((), ())), preferred_element_type=jnp.float32
        )
        update = lax.psum_scatter(
            partial_value.astype(jnp.bfloat16), "mp", scatter_dimension=1, tiled=True
        ).astype(jnp.float32)
        carried = (carried.astype(jnp.float32) + update).astype(jnp.bfloat16)
        if section_step >= sections - 1:
            finished.append(carried)
    returned_rows = broadcast(jnp.stack(finished), "section", sections - 1)
    final_hidden = lax.dynamic_index_in_dim(returned_rows, section_here, 0, keepdims=False)
    columns = row_grads.shape[1]
    picker = ((target == group_here)[:, None] & (position[:, None] == positions[None, :])).astype(
        jnp.bfloat16
    )
    outgoing = jnp.dot(picker, row_grads, preferred_element_type=jnp.float32).astype(jnp.bfloat16)
    outgoing = outgoing.reshape(dp_count, section_rows // dp_count, columns)
    returned = lax.all_to_all(
        lax.all_to_all(outgoing, "dp", split_axis=0, concat_axis=0, tiled=True),
        "mp",
        split_axis=1,
        concat_axis=2,
        tiled=True,
    )
    merged_grads = jnp.sum(returned.astype(jnp.float32), axis=0).astype(jnp.bfloat16)
    return (final_hidden, merged_grads)


def solution(mesh):
    in_specs = (
        P(("section", "dp", "mp"), None),
        P(("section", "dp", "mp"), None),
        P(),
        P(),
        P(),
        P(),
        P("dp", "mp"),
        P(("section", "dp", "mp"), None),
        P(("section", "dp"), "mp"),
        P(("section", "dp"), None),
        P("section", None),
        P("section", "dp", "mp"),
        P("section", "dp", "mp"),
        P(("section", "dp"), "mp"),
    )
    out_specs = (P(("section", "dp"), "mp"), P(("section", "dp", "mp"), None))
    return jax.shard_map(shards, mesh=mesh, in_specs=in_specs, out_specs=out_specs, check_vma=False)
```

profile of v0, /device:TPU:0, one launch (start us, length us, event | category | flops | bytes accessed | tf_op | source)
XLA Modules:
  0.0 799.6 jit_solution(8067572202809848577)
XLA Ops:
  9.6 6.6 convolution_convert_fusion.1
  16.2 3.1 reshape.446
  23.9 2.4 fusion.64
  34.4 24.9 %all-reduce = s32[1024]{0:T(1024)S(1)} all-reduce(s32[1024]{0:T(1024)S(1)} %bitcast_dynamic-update-slice_fusion), channel_id=1, replica_groups=mesh['section'=2,'dp'=16,'mp'=4] {'dp','mp'}, use_global_device_ids=true, to_apply=%add | all-reduce | flops 1024 | bytes 8192 | tf_op jit(solution)/shard_map/squeeze | solution.py:120
  60.4 60.5 %all-gather.9.cloned.1.call-done = bf16[1024,5120]{1,0:T(8,128)(2,1)} async-done(((bf16[16,5120]{1,0:T(8,128)(2,1)}), bf16[1024,5120]{1,0:T(8,128)(2,1)}) %all-gather.9.cloned.1.call-update) | async-done | bytes 10485776 | tf_op jit(solution)/shard_map/all_gather | solution.py:117
  120.9 10.7 %convolution_convert_fusion = bf16[2048,2048]{1,0:T(8,128)(2,1)} fusion(bf16[320,2048]{1,0:T(8,128)(2,1)} %param.20, s32[1024]{0:T(1024)S(1)} %get-tuple-element.7, bf16[1024,5120]{1,0:T(8,128)(2,1)} %all-gather.9.cloned.1.call-done, s32[]{:T(128)S(6)} %select_n.69), kind=kOutput, calls=%fused_computation.18 | convolution fusion | flops 4033478656 | bytes 10489860 | tf_op jit(solution)/shard_map/dot_general | solution.py:137
  132.4 83.8 %reduce-scatter.5.cloned.1.call-done = bf16[128,2048]{1,0:T(8,128)(2,1)} async-done(((bf16[2048,2048]{1,0:T(8,128)(2,1)}), bf16[128,2048]{1,0:T(8,128)(2,1)}) %reduce-scatter.5.cloned.1.call-update) | async-done | bytes 524304 | tf_op jit(solution)/shard_map/reduce_scatter | solution.py:136
  218.3 11.4 %all-gather.11.cloned.1.call-done = bf16[256,2048]{1,0:T(8,128)(2,1)} async-done(((bf16[128,2048]{1,0:T(8,128)(2,1)}), bf16[256,2048]{1,0:T(8,128)(2,1)}) %all-gather.11.cloned.1.call-update) | async-done | bytes 1048592 | tf_op jit(solution)/shard_map/all_gather | solution.py:157
  232.8 2.2 all-gather
  235.4 28.8 %all-gather.13.cloned.1.call-done = bf16[128,8192]{1,0:T(8,128)(2,1)} async-done(((bf16[128,2048]{1,0:T(8,128)(2,1)}), bf16[128,8192]{1,0:T(8,128)(2,1)}) %all-gather.13.cloned.1.call-update) | async-done | bytes 2097168 | tf_op jit(solution)/shard_map/all_gather | solution.py:171
  266.3 132.4 %all-gather.15.cloned.1.call-done = bf16[1,8192,1280]{2,1,0:T(8,128)(2,1)} async-done(((bf16[1,512,1280]{2,1,0:T(8,128)(2,1)}), bf16[1,8192,1280]{2,1,0:T(8,128)(2,1)}) %all-gather.15.cloned.1.call-update) | async-done | bytes 20971536 | tf_op jit(solution)/shard_map/all_gather | solution.py:146
  398.7 10.6 %fusion.35 = bf16[128,1280]{1,0:T(8,128)(2,1)S(1)} fusion(bf16[1,8192,1280]{2,1,0:T(8,128)(2,1)} %all-gather.15.cloned.1.call-done, bf16[128,8192]{1,0:T(8,128)(2,1)} %all-gather.13.cloned.1.call-done, f32[8192]{0:T(1024)S(1)} %bitcast.203, f32[128]{0:T(128)S(1)} %add_rsqrt_fusion.2), kind=kOutput, calls=%fused_computation.41 | convolution fusion | flops 2688712704 | bytes 23429632 | tf_op jit(solution)/shard_map/dot_general | solution.py:173
  410.1 101.6 %all-gather.17.cloned.1.call-done = bf16[1,8192,1024]{2,1,0:T(8,128)(2,1)} async-done(((bf16[1,512,1024]{2,1,0:T(8,128)(2,1)}), bf16[1,8192,1024]{2,1,0:T(8,128)(2,1)}) %all-gather.17.cloned.1.call-update) | async-done | bytes 16777232 | tf_op jit(solution)/shard_map/all_gather | solution.py:147
  511.7 12.8 %fusion.13 = bf16[128,8192]{1,0:T(8,128)(2,1)} fusion(bf16[128,1024]{0,1:T(8,128)(2,1)S(1)} %bitcast.197, bf16[1,8192,1024]{2,1,0:T(8,128)(2,1)} %all-gather.17.cloned.1.call-done), kind=kOutput, calls=%fused_computation.13 | convolution fusion | flops 2148532224 | bytes 19136512 | tf_op jit(solution)/shard_map/dot_general | solution.py:175
  524.6 29.7 %reduce-scatter.7.cloned.1.call-done = bf16[128,2048]{1,0:T(8,128)(2,1)} async-done(((bf16[128,8192]{1,0:T(8,128)(2,1)}), bf16[128,2048]{1,0:T(8,128)(2,1)}) %reduce-scatter.7.cloned.1.call-update) | async-done | bytes 524304 | tf_op jit(solution)/shard_map/reduce_scatter | solution.py:178
  559.8 2.5 collective-permute-start.1
  563.2 27.3 %all-gather.19.cloned.1.call-done = bf16[128,8192]{1,0:T(8,128)(2,1)} async-done(((bf16[128,2048]{1,0:T(8,128)(2,1)}), bf16[128,8192]{1,0:T(8,128)(2,1)}) %all-gather.19.cloned.1.call-update) | async-done | bytes 2097168 | tf_op jit(solution)/shard_map/all_gather | solution.py:171
  592.6 10.6 %fusion.38 = bf16[128,1280]{1,0:T(8,128)(2,1)S(1)} fusion(bf16[1,8192,1280]{2,1,0:T(8,128)(2,1)} %all-gather.15.cloned.1.call-done, bf16[128,8192]{1,0:T(8,128)(2,1)} %all-gather.19.cloned.1.call-done, f32[128]{0:T(128)S(1)} %add_rsqrt_fusion.1, f32[8192]{0:T(1024)S(1)} %bitcast.204), kind=kOutput, calls=%fused_computation.42 | convolution fusion | flops 2688712704 | bytes 23429632 | tf_op jit(solution)/shard_map/dot_general | solution.py:173
  604.0 12.8 %fusion.16 = bf16[128,8192]{1,0:T(8,128)(2,1)} fusion(bf16[128,1024]{0,1:T(8,128)(2,1)S(1)} %bitcast.199, bf16[1,8192,1024]{2,1,0:T(8,128)(2,1)} %all-gather.17.cloned.1.call-done), kind=kOutput, calls=%fused_computation.14 | convolution fusion | flops 2148532224 | bytes 19136512 | tf_op jit(solution)/shard_map/dot_general | solution.py:175
  616.9 29.9 %reduce-scatter.9.cloned.1.call-done = bf16[128,2048]{1,0:T(8,128)(2,1)} async-done(((bf16[128,8192]{1,0:T(8,128)(2,1)}), bf16[128,2048]{1,0:T(8,128)(2,1)}) %reduce-scatter.9.cloned.1.call-update) | async-done | bytes 524304 | tf_op jit(solution)/shard_map/reduce_scatter | solution.py:178
  652.1 3.1 convolution_convert_fusion.2
  655.2 6.9 all-to-all-start
  662.1 2.2 collective-permute-start.3
  665.3 17.6 %all-gather.21.cloned.1.call-done = bf16[128,8192]{1,0:T(8,128)(2,1)} async-done(((bf16[128,2048]{1,0:T(8,128)(2,1)}), bf16[128,8192]{1,0:T(8,128)(2,1)}) %all-gather.21.cloned.1.call-update) | async-done | bytes 2097168 | tf_op jit(solution)/shard_map/all_gather | solution.py:171
  685.0 10.6 %fusion.41 = bf16[128,1280]{1,0:T(8,128)(2,1)S(1)} fusion(bf16[1,8192,1280]{2,1,0:T(8,128)(2,1)} %all-gather.15.cloned.1.call-done, bf16[128,8192]{1,0:T(8,128)(2,1)} %all-gather.21.cloned.1.call-done, f32[128]{0:T(128)S(1)} %add_rsqrt_fusion, f32[8192]{0:T(1024)S(1)} %bitcast.205), kind=kOutput, calls=%fused_computation.43 | convolution fusion | flops 2688712704 | bytes 23429632 | tf_op jit(solution)/shard_map/dot_general | solution.py:173
  696.5 12.8 %fusion.19 = bf16[128,8192]{1,0:T(8,128)(2,1)} fusion(bf16[128,1024]{0,1:T(8,128)(2,1)S(1)} %bitcast.198, bf16[1,8192,1024]{2,1,0:T(8,128)(2,1)} %all-gather.17.cloned.1.call-done), kind=kOutput, calls=%fused_computation.15 | convolution fusion | flops 2148532224 | bytes 19136512 | tf_op jit(solution)/shard_map/dot_general | solution.py:175
  709.3 16.7 %all-to-all-done = bf16[16,64,2048]{2,1,0:T(8,128)(2,1)} async-done(((bf16[16,64,2048]{2,1,0:T(8,128)(2,1)}), bf16[16,64,2048]{2,1,0:T(8,128)(2,1)}, u32[]{:S(2)}, u32[]{:S(2)}) %all-to-all-start) | async-done | bytes 4194336 | tf_op jit(solution)/shard_map/all_to_all | solution.py:193
  726.0 6.5 copy.122
  732.5 5.0 all-to-all-start.1
  740.4 2.4 maximum_select_fusion
  742.8 43.2 %all-to-all-done.1 = bf16[16,64,2048]{2,0,1:T(8,128)(2,1)} async-done(((bf16[16,64,2048]{2,0,1:T(8,128)(2,1)}), bf16[16,64,2048]{2,0,1:T(8,128)(2,1)}, u32[]{:S(2)}, u32[]{:S(2)}) %all-to-all-start.1) | async-done | bytes 4194336 | tf_op jit(solution)/shard_map/all_to_all | solution.py:192
  786.0 3.9 reduce_sum.188
  (129 shorter events, 48.7 us)
Async XLA Ops:
  7.2 22.9 %copy-start = (bf16[1280,1280]{1,0:T(8,128)(2,1)S(1)}, bf16[1280,1280]{1,0:T(8,128)(2,1)}, u32[]{:S(2)}) copy-start(bf16[1280,1280]{1,0:T(8,128)(2,1)} %param.18) | copy-start | bytes 9830404
  7.2 113.7 %all-gather.9.cloned.1.call-start = ((), (), s32[]{:S(2)}) async-start(), calls=%async_computation.6 | async-start | bytes 10649600 | tf_op jit(solution)/shard_map/all_gather | solution.py:117
  9.6 11.7 %copy-start.13 = (s32[1,3]{1,0:T(1,128)S(1)}, s32[1,3]{1,0:T(1,128)}, u32[]{:S(2)}) copy-start(s32[1,3]{1,0:T(1,128)} %param.15) | copy-start | bytes 40
  16.2 13.9 %copy-start.3 = (bf16[64,1280]{1,0:T(8,128)(2,1)S(1)}, bf16[64,1280]{1,0:T(8,128)(2,1)}, u32[]{:S(2)}) copy-start(bf16[64,1280]{1,0:T(8,128)(2,1)} %param.14) | copy-start | bytes 491524
  23.1 8.9 %copy-start.10 = (f32[1280]{0:T(1024)S(1)}, f32[1280]{0:T(1024)}, u32[]{:S(2)}) copy-start(f32[1280]{0:T(1024)} %param.19) | copy-start | bytes 15364
  23.9 9.1 %copy-start.16 = (u32[128]{0:T(128)S(1)}, u32[128]{0:T(128)}, u32[]{:S(2)}) copy-start(u32[128]{0:T(128)} %constant.73) | copy-start | bytes 1540
  23.9 10.3 %copy-start.14 = (s32[16,1]{0,1:T(1,128)S(1)}, s32[16,1]{0,1:T(1,128)}, u32[]{:S(2)}) copy-start(s32[16,1]{0,1:T(1,128)} %param.21) | copy-start | bytes 196
  32.9 183.3 %reduce-scatter.5.cloned.1.call-start = ((), (), s32[]{:S(2)}) async-start(), calls=%async_computation.7 | async-start | bytes 8912896 | tf_op jit(solution)/shard_map/reduce_scatter | solution.py:136
  131.6 84.6 %copy-start.9 = (bf16[128,2048]{1,0:T(8,128)(2,1)S(1)}, bf16[128,2048]{1,0:T(8,128)(2,1)}, u32[]{:S(2)}) copy-start(bf16[128,2048]{1,0:T(8,128)(2,1)} %param.22) | copy-start | bytes 1572868
  131.7 101.1 %copy-start.11 = (s32[1,3]{1,0:T(1,128)S(1)}, s32[1,3]{1,0:T(1,128)}, u32[]{:S(2)}) copy-start(s32[1,3]{1,0:T(1,128)} %param.23) | copy-start | bytes 40
  131.7 267.0 %copy-start.12 = (f32[1,8192]{1,0:T(1,128)S(1)}, f32[1,8192]{1,0:T(1,128)}, u32[]{:S(2)}) copy-start(f32[1,8192]{1,0:T(1,128)} %param.24) | copy-start | bytes 98308
  131.7 98.0 %all-gather.11.cloned.1.call-start = ((), (), s32[]{:S(2)}) async-start(), calls=%async_computation.8 | async-start | bytes 1572864 | tf_op jit(solution)/shard_map/all_gather | solution.py:157
  218.2 46.0 %all-gather.13.cloned.1.call-start = ((), (), s32[]{:S(2)}) async-start(), calls=%async_computation.9 | async-start | bytes 2621440 | tf_op jit(solution)/shard_map/all_gather | solution.py:171
  231.6 167.1 %all-gather.15.cloned.1.call-start = ((), (), s32[]{:S(2)}) async-start(), calls=%async_computation.10 | async-start | bytes 22282240 | tf_op jit(solution)/shard_map/all_gather | solution.py:146
  232.2 279.5 %all-gather.17.cloned.1.call-start = ((), (), s32[]{:S(2)}) async-start(), calls=%async_computation.11 | async-start | bytes 17825792 | tf_op jit(solution)/shard_map/all_gather | solution.py:147
  232.7 321.6 %reduce-scatter.7.cloned.1.call-start = ((), (), s32[]{:S(2)}) async-start(), calls=%async_computation.12 | async-start | bytes 2621440 | tf_op jit(solution)/shard_map/reduce_scatter | solution.py:178
  511.7 42.6 %copy-start.4 = (bf16[256,2048]{1,0:T(8,128)(2,1)S(1)}, bf16[256,2048]{1,0:T(8,128)(2,1)}, u32[]{:S(2)}) copy-start(bf16[256,2048]{1,0:T(8,128)(2,1)} %all-gather.11.cloned.1.call-done) | copy-start | bytes 3145732
  524.5 66.0 %all-gather.19.cloned.1.call-start = ((), (), s32[]{:S(2)}) async-start(), calls=%async_computation.13 | async-start | bytes 2621440 | tf_op jit(solution)/shard_map/all_gather | solution.py:171
  555.5 3.3 collective-permute-start
  559.7 87.1 %reduce-scatter.9.cloned.1.call-start = ((), (), s32[]{:S(2)}) async-start(), calls=%async_computation.14 | async-start | bytes 2621440 | tf_op jit(solution)/shard_map/reduce_scatter | solution.py:178
  559.8 3.1 collective-permute-start.1
  604.0 42.7 %copy-start.2 = (bf16[128,2048]{1,0:T(8,128)(2,1)S(1)}, bf16[128,2048]{1,0:T(8,128)(2,1)}, u32[]{:S(2)}) copy-start(bf16[128,2048]{1,0:T(8,128)(2,1)} %slice_select_fusion.1) | copy-start | bytes 1572868
  616.8 35.3 %copy-start.8 = (bf16[128,2048]{1,0:T(8,128)(2,1)S(1)}, bf16[128,2048]{1,0:T(8,128)(2,1)}, u32[]{:S(2)}) copy-start(bf16[128,2048]{1,0:T(8,128)(2,1)} %param.27) | copy-start | bytes 1572868
  616.9 66.1 %all-gather.21.cloned.1.call-start = ((), (), s32[]{:S(2)}) async-start(), calls=%async_computation.15 | async-start | bytes 2621440 | tf_op jit(solution)/shard_map/all_gather | solution.py:171
  647.9 7.3 copy-start.5
  648.0 3.3 collective-permute-start.2
  655.2 70.8 %all-to-all-start = ((bf16[16,64,2048]{2,1,0:T(8,128)(2,1)}), bf16[16,64,2048]{2,1,0:T(8,128)(2,1)}, u32[]{:S(2)}, u32[]{:S(2)}) async-start(bf16[16,64,2048]{2,1,0:T(8,128)(2,1)} %bitcast.188), calls=%async_computation.4 | async-start | bytes 8388608 | tf_op jit(solution)/shard_map/all_to_all | solution.py:193
  662.1 77.1 %reduce-scatter.11.cloned.1.call-start = ((), (), s32[]{:S(2)}) async-start(), calls=%async_computation.16 | async-start | bytes 2621440 | tf_op jit(solution)/shard_map/reduce_scatter | solution.py:178
  662.1 2.8 collective-permute-start.3
  732.5 53.5 %all-to-all-start.1 = ((bf16[16,64,2048]{2,0,1:T(8,128)(2,1)}), bf16[16,64,2048]{2,0,1:T(8,128)(2,1)}, u32[]{:S(2)}, u32[]{:S(2)}) async-start(bf16[16,64,2048]{2,0,1:T(8,128)(2,1)} %copy.122), calls=%async_computation.5 | async-start | bytes 8388608 | tf_op jit(solution)/shard_map/all_to_all | solution.py:192
  737.5 53.2 %all-reduce.3.cloned.1.call-start = ((), (), s32[]{:S(2)}) async-start(), calls=%async_computation.17 | async-start | bytes 2097152 | tf_op jit(solution)/shard_map/psum | solution.py:25
  740.4 52.1 %copy-start.1 = (bf16[1280,1280]{1,0:T(8,128)(2,1)S(1)}, bf16[1280,1280]{1,0:T(8,128)(2,1)}, u32[]{:S(2)}) copy-start(bf16[1280,1280]{1,0:T(8,128)(2,1)} %param.18) | copy-start | bytes 9830404
  (3 other events, 8.3 us)
Sparse Core Ops, SparseCore 0:
  33.0 87.8 all-gather.8
  131.8 84.4 reduce-scatter.4
  218.5 11.1 all-gather.10
  231.8 32.4 all-gather.12
  266.2 132.4 all-gather.14
  400.7 110.9 all-gather.16
  524.7 29.5 reduce-scatter.6
  559.8 30.6 all-gather.18
  617.0 29.7 reduce-scatter.8
  652.2 30.6 all-gather.20
  709.4 29.7 reduce-scatter.10
  742.9 26.6 all-reduce.2
where the time goes:
time: 808 us; the launch traced here: 800 us
  waiting for transfers between devices  590 us (73%)
  matrix products  97.5 us (12%)
  blocking collectives  27.2 us (3%)
  other arithmetic  27.1 us (3%)
  local copies, waits for them, and re-layouts  21.7 us (3%)
  starting transfers between devices  20.7 us (3%)
  between operations  15.5 us (2%)
    all_gather x1, waiting for transfers between devices, shards(): lax.all_gather(w_qkv, 'dp', axis=1, tiled=True)  132 us
    all_gather x1, waiting for transfers between devices, shards(): lax.all_gather(wo_t, 'dp', axis=1, tiled=True)  102 us
    reduce_scatter x1, waiting for transfers between devices, shards(): lax.psum_scatter(jnp.dot(picked, w_merge, preferred_element_type=jnp.floa...  83.8 us
    all_gather x3, waiting for transfers between devices, shards(): features = lax.all_gather(carried, 'mp', axis=1, tiled=True)  73.8 us
    reduce_scatter x3, waiting for transfers between devices, shards(): lax.psum_scatter(partial_value.astype(jnp.bfloat16), 'mp', scatter_dimens...  61.3 us
    all_gather x1, waiting for transfers between devices, shards(): lax.all_gather(merged, ('dp', 'mp'), axis=0, tiled=True)  60.5 us
    all_to_all x1, waiting for transfers between devices, shards(): lax.all_to_all(lax.all_to_all(outgoing, 'dp', split_axis=0, concat_axis=0...  43.2 us
    dot_general x3, matrix products, shards(): lax.dot_general(attended, out_weight, (((1,), (1,)), ((), ())), preferred...  38.4 us
  transfers between devices with their start and end apart: 18, of which 17 were waited for; matrix products, arithmetic and copies ran while one was open for 8% of the time, Pallas kernels for 0%

commit v1 on v0

--- a/solution.py
+++ b/solution.py
@@ -144,7 +144,9 @@
     entry_rows = jnp.where((positions < present)[:, None], image_rows, text)
     gathered = (
         lax.all_gather(w_qkv, "dp", axis=1, tiled=True),
-        lax.all_gather(wo_t, "dp", axis=1, tiled=True),
+        jnp.concatenate(
+            lax.all_to_all(jnp.stack([wo_t] * lax.axis_size("dp")), "dp", 0, 0), axis=1
+        ),
     )
     qkv_weight = gathered[0][0]
     out_weight = gathered[1][0]

time: 808 us -> 907 us (1.12)
  waiting for transfers between devices: 590 us -> 676 us
    all_gather x1, waiting for transfers between devices: 132 us -> 318 us  [shards(): lax.all_gather(w_qkv, 'dp', axis=1, tiled=True)]
    all_gather x1 -> x0, waiting for transfers between devices: 102 us -> none  [shards(): lax.all_gather(wo_t, 'dp', axis=1, tiled=True)]
    reduce_scatter x3, waiting for transfers between devices: 61.3 us -> 76.3 us  [shards(): lax.psum_scatter(partial_value.astype(jnp.bfloat16), 'mp', scatter_dimens...]
    all_gather x3, waiting for transfers between devices: 73.8 us -> 61.3 us  [shards(): features = lax.all_gather(carried, 'mp', axis=1, tiled=True)]
  transfers between devices with their start and end apart: 18 -> 18, of which waited for: 17 -> 16; matrix products, arithmetic and copies ran while one was open for 8% -> 7% of each run, Pallas kernels for 0% -> 0%
where the time goes in v1:
time: 907 us; the launch traced here: 898 us
  waiting for transfers between devices  676 us (75%)
  matrix products  97.5 us (11%)
  local copies, waits for them, and re-layouts  27.7 us (3%)
  starting transfers between devices  27.7 us (3%)
  blocking collectives  27.2 us (3%)
  other arithmetic  27.1 us (3%)
  between operations  15.2 us (2%)
    all_gather x1, waiting for transfers between devices, shards(): lax.all_gather(w_qkv, 'dp', axis=1, tiled=True)  318 us
    reduce_scatter x1, waiting for transfers between devices, shards(): lax.psum_scatter(jnp.dot(picked, w_merge, preferred_element_type=jnp.floa...  83.8 us
    reduce_scatter x3, waiting for transfers between devices, shards(): lax.psum_scatter(partial_value.astype(jnp.bfloat16), 'mp', scatter_dimens...  76.3 us
    all_gather x3, waiting for transfers between devices, shards(): features = lax.all_gather(carried, 'mp', axis=1, tiled=True)  61.3 us
    all_gather x1, waiting for transfers between devices, shards(): lax.all_gather(merged, ('dp', 'mp'), axis=0, tiled=True)  60.5 us
    all_to_all x1, waiting for transfers between devices, shards(): lax.all_to_all(lax.all_to_all(outgoing, 'dp', split_axis=0, concat_axis=0...  43.2 us
    dot_general x3, matrix products, shards(): lax.dot_general(attended, out_weight, (((1,), (1,)), ((), ())), preferred...  38.4 us
    dot_general x3, matrix products, shards(): projected = jnp.dot(normed, qkv_weight, preferred_element_type=jnp.float32)  31.7 us
  transfers between devices with their start and end apart: 18, of which 16 were waited for; matrix products, arithmetic and copies ran while one was open for 7% of the time, Pallas kernels for 0%

profile of v1, /device:TPU:0, one launch (start us, length us, event | category | flops | bytes accessed | tf_op | source)
XLA Modules:
  0.0 898.1 jit_solution(7105874098749968875)
XLA Ops:
  9.6 6.6 convolution_convert_fusion.4
  16.2 3.1 reshape.449
  23.9 2.4 fusion.49
  34.4 24.9 %all-reduce = s32[1024]{0:T(1024)S(1)} all-reduce(s32[1024]{0:T(1024)S(1)} %bitcast_dynamic-update-slice_fusion), channel_id=1, replica_groups=mesh['section'=2,'dp'=16,'mp'=4] {'dp','mp'}, use_global_device_ids=true, to_apply=%add | all-reduce | flops 1024 | bytes 8192 | tf_op jit(solution)/shard_map/squeeze | solution.py:120
  60.4 60.5 %all-gather.8.cloned.1.call-done = bf16[1024,5120]{1,0:T(8,128)(2,1)} async-done(((bf16[16,5120]{1,0:T(8,128)(2,1)}), bf16[1024,5120]{1,0:T(8,128)(2,1)}) %all-gather.8.cloned.1.call-update) | async-done | bytes 10485776 | tf_op jit(solution)/shard_map/all_gather | solution.py:117
  120.9 10.7 %convolution_convert_fusion.3 = bf16[2048,2048]{1,0:T(8,128)(2,1)} fusion(bf16[320,2048]{1,0:T(8,128)(2,1)} %param.20, s32[1024]{0:T(1024)S(1)} %get-tuple-element.7, bf16[1024,5120]{1,0:T(8,128)(2,1)} %all-gather.8.cloned.1.call-done, s32[]{:T(128)S(6)} %select_n.69), kind=kOutput, calls=%fused_computation.12 | convolution fusion | flops 4033478656 | bytes 10489860 | tf_op jit(solution)/shard_map/dot_general | solution.py:137
  132.5 83.8 %reduce-scatter.5.cloned.1.call-done = bf16[128,2048]{1,0:T(8,128)(2,1)} async-done(((bf16[2048,2048]{1,0:T(8,128)(2,1)}), bf16[128,2048]{1,0:T(8,128)(2,1)}) %reduce-scatter.5.cloned.1.call-update) | async-done | bytes 524304 | tf_op jit(solution)/shard_map/reduce_scatter | solution.py:136
  218.3 11.4 %all-gather.10.cloned.1.call-done = bf16[256,2048]{1,0:T(8,128)(2,1)} async-done(((bf16[128,2048]{1,0:T(8,128)(2,1)}), bf16[256,2048]{1,0:T(8,128)(2,1)}) %all-gather.10.cloned.1.call-update) | async-done | bytes 1048592 | tf_op jit(solution)/shard_map/all_gather | solution.py:159
  232.2 6.0 stack.8
  238.2 7.1 all-to-all-start
  245.3 2.2 all-gather
  247.9 16.3 %all-gather.12.cloned.1.call-done = bf16[128,8192]{1,0:T(8,128)(2,1)} async-done(((bf16[128,2048]{1,0:T(8,128)(2,1)}), bf16[128,8192]{1,0:T(8,128)(2,1)}) %all-gather.12.cloned.1.call-update) | async-done | bytes 2097168 | tf_op jit(solution)/shard_map/all_gather | solution.py:173
  266.3 317.7 %all-gather.14.cloned.1.call-done = bf16[1,8192,1280]{2,1,0:T(8,128)(2,1)} async-done(((bf16[1,512,1280]{2,1,0:T(8,128)(2,1)}), bf16[1,8192,1280]{2,1,0:T(8,128)(2,1)}) %all-gather.14.cloned.1.call-update) | async-done | bytes 20971536 | tf_op jit(solution)/shard_map/all_gather | solution.py:146
  584.0 10.6 %fusion.20 = bf16[128,1280]{1,0:T(8,128)(2,1)S(1)} fusion(bf16[1,8192,1280]{2,1,0:T(8,128)(2,1)} %all-gather.14.cloned.1.call-done, bf16[128,8192]{1,0:T(8,128)(2,1)} %all-gather.12.cloned.1.call-done, f32[8192]{0:T(1024)S(1)} %bitcast.196, f32[128]{0:T(128)S(1)} %add_rsqrt_fusion.2), kind=kOutput, calls=%fused_computation.35 | convolution fusion | flops 2688712704 | bytes 23429632 | tf_op jit(solution)/shard_map/dot_general | solution.py:175
  595.4 12.8 %convolution_convert_fusion.2 = bf16[128,8192]{1,0:T(8,128)(2,1)} fusion(bf16[128,1024]{0,1:T(8,128)(2,1)S(1)} %bitcast.190, bf16[8192,1024]{1,0:T(8,128)(2,1)} %bitcast.27), kind=kOutput, calls=%fused_computation.9 | convolution fusion | flops 2148532224 | bytes 19136512 | tf_op jit(solution)/shard_map/dot_general | solution.py:177
  608.3 44.8 %reduce-scatter.7.cloned.1.call-done = bf16[128,2048]{1,0:T(8,128)(2,1)} async-done(((bf16[128,8192]{1,0:T(8,128)(2,1)}), bf16[128,2048]{1,0:T(8,128)(2,1)}) %reduce-scatter.7.cloned.1.call-update) | async-done | bytes 524304 | tf_op jit(solution)/shard_map/reduce_scatter | solution.py:180
  658.5 2.5 collective-permute-start.1
  662.0 27.3 %all-gather.16.cloned.1.call-done = bf16[128,8192]{1,0:T(8,128)(2,1)} async-done(((bf16[128,2048]{1,0:T(8,128)(2,1)}), bf16[128,8192]{1,0:T(8,128)(2,1)}) %all-gather.16.cloned.1.call-update) | async-done | bytes 2097168 | tf_op jit(solution)/shard_map/all_gather | solution.py:173
  691.4 10.6 %fusion.23 = bf16[128,1280]{1,0:T(8,128)(2,1)S(1)} fusion(bf16[1,8192,1280]{2,1,0:T(8,128)(2,1)} %all-gather.14.cloned.1.call-done, bf16[128,8192]{1,0:T(8,128)(2,1)} %all-gather.16.cloned.1.call-done, f32[128]{0:T(128)S(1)} %add_rsqrt_fusion.1, f32[8192]{0:T(1024)S(1)} %bitcast.197), kind=kOutput, calls=%fused_computation.36 | convolution fusion | flops 2688712704 | bytes 23429632 | tf_op jit(solution)/shard_map/dot_general | solution.py:175
  702.8 12.8 %convolution_convert_fusion.1 = bf16[128,8192]{1,0:T(8,128)(2,1)} fusion(bf16[128,1024]{0,1:T(8,128)(2,1)S(1)} %bitcast.192, bf16[8192,1024]{1,0:T(8,128)(2,1)} %bitcast.27), kind=kOutput, calls=%fused_computation.8 | convolution fusion | flops 2148532224 | bytes 19136512 | tf_op jit(solution)/shard_map/dot_general | solution.py:177
  715.7 29.9 %reduce-scatter.9.cloned.1.call-done = bf16[128,2048]{1,0:T(8,128)(2,1)} async-done(((bf16[128,8192]{1,0:T(8,128)(2,1)}), bf16[128,2048]{1,0:T(8,128)(2,1)}) %reduce-scatter.9.cloned.1.call-update) | async-done | bytes 524304 | tf_op jit(solution)/shard_map/reduce_scatter | solution.py:180
  750.9 3.1 convolution_convert_fusion.5
  754.0 6.9 all-to-all-start.1
  764.1 17.6 %all-gather.18.cloned.1.call-done = bf16[128,8192]{1,0:T(8,128)(2,1)} async-done(((bf16[128,2048]{1,0:T(8,128)(2,1)}), bf16[128,8192]{1,0:T(8,128)(2,1)}) %all-gather.18.cloned.1.call-update) | async-done | bytes 2097168 | tf_op jit(solution)/shard_map/all_gather | solution.py:173
  783.8 10.6 %fusion.26 = bf16[128,1280]{1,0:T(8,128)(2,1)S(1)} fusion(bf16[1,8192,1280]{2,1,0:T(8,128)(2,1)} %all-gather.14.cloned.1.call-done, bf16[128,8192]{1,0:T(8,128)(2,1)} %all-gather.18.cloned.1.call-done, f32[128]{0:T(128)S(1)} %add_rsqrt_fusion, f32[8192]{0:T(1024)S(1)} %bitcast.198), kind=kOutput, calls=%fused_computation.37 | convolution fusion | flops 2688712704 | bytes 23429632 | tf_op jit(solution)/shard_map/dot_general | solution.py:175
  795.2 12.8 %convolution_convert_fusion = bf16[128,8192]{1,0:T(8,128)(2,1)} fusion(bf16[128,1024]{0,1:T(8,128)(2,1)S(1)} %bitcast.191, bf16[8192,1024]{1,0:T(8,128)(2,1)} %bitcast.27), kind=kOutput, calls=%fused_computation.7 | convolution fusion | flops 2148532224 | bytes 19136512 | tf_op jit(solution)/shard_map/dot_general | solution.py:177
  808.1 16.7 %all-to-all-done.1 = bf16[16,64,2048]{2,1,0:T(8,128)(2,1)} async-done(((bf16[16,64,2048]{2,1,0:T(8,128)(2,1)}), bf16[16,64,2048]{2,1,0:T(8,128)(2,1)}, u32[]{:S(2)}, u32[]{:S(2)}) %all-to-all-start.1) | async-done | bytes 4194336 | tf_op jit(solution)/shard_map/all_to_all | solution.py:195
  824.8 6.5 copy.122
  831.3 5.0 all-to-all-start.2
  839.2 2.4 maximum_select_fusion
  841.6 43.2 %all-to-all-done.2 = bf16[16,64,2048]{2,0,1:T(8,128)(2,1)} async-done(((bf16[16,64,2048]{2,0,1:T(8,128)(2,1)}), bf16[16,64,2048]{2,0,1:T(8,128)(2,1)}, u32[]{:S(2)}, u32[]{:S(2)}) %all-to-all-start.2) | async-done | bytes 4194336 | tf_op jit(solution)/shard_map/all_to_all | solution.py:194
  884.8 3.9 reduce_sum.188
  (131 shorter events, 50.4 us)
Async XLA Ops:
  7.2 22.9 %copy-start = (bf16[1280,1280]{1,0:T(8,128)(2,1)S(1)}, bf16[1280,1280]{1,0:T(8,128)(2,1)}, u32[]{:S(2)}) copy-start(bf16[1280,1280]{1,0:T(8,128)(2,1)} %param.18) | copy-start | bytes 9830404
  7.2 113.7 %all-gather.8.cloned.1.call-start = ((), (), s32[]{:S(2)}) async-start(), calls=%async_computation.7 | async-start | bytes 10649600 | tf_op jit(solution)/shard_map/all_gather | solution.py:117
  9.6 11.7 %copy-start.14 = (s32[1,3]{1,0:T(1,128)S(1)}, s32[1,3]{1,0:T(1,128)}, u32[]{:S(2)}) copy-start(s32[1,3]{1,0:T(1,128)} %param.15) | copy-start | bytes 40
  16.2 13.9 %copy-start.3 = (bf16[64,1280]{1,0:T(8,128)(2,1)S(1)}, bf16[64,1280]{1,0:T(8,128)(2,1)}, u32[]{:S(2)}) copy-start(bf16[64,1280]{1,0:T(8,128)(2,1)} %param.14) | copy-start | bytes 491524
  23.1 8.9 copy-start.11
  23.9 9.1 %copy-start.17 = (u32[128]{0:T(128)S(1)}, u32[128]{0:T(128)}, u32[]{:S(2)}) copy-start(u32[128]{0:T(128)} %constant.73) | copy-start | bytes 1540
  23.9 10.3 %copy-start.15 = (s32[16,1]{0,1:T(1,128)S(1)}, s32[16,1]{0,1:T(1,128)}, u32[]{:S(2)}) copy-start(s32[16,1]{0,1:T(1,128)} %param.21) | copy-start | bytes 196
  32.9 183.3 %reduce-scatter.5.cloned.1.call-start = ((), (), s32[]{:S(2)}) async-start(), calls=%async_computation.8 | async-start | bytes 8912896 | tf_op jit(solution)/shard_map/reduce_scatter | solution.py:136
  131.6 84.6 %copy-start.10 = (bf16[128,2048]{1,0:T(8,128)(2,1)S(1)}, bf16[128,2048]{1,0:T(8,128)(2,1)}, u32[]{:S(2)}) copy-start(bf16[128,2048]{1,0:T(8,128)(2,1)} %param.22) | copy-start | bytes 1572868
  131.7 100.5 %copy-start.8 = (bf16[1,512,1024]{2,1,0:T(8,128)(2,1)S(1)}, bf16[1,512,1024]{2,1,0:T(8,128)(2,1)}, u32[]{:S(2)}) copy-start(bf16[1,512,1024]{2,1,0:T(8,128)(2,1)} %param.26) | copy-start | bytes 3145732
  131.7 98.0 %all-gather.10.cloned.1.call-start = ((), (), s32[]{:S(2)}) async-start(), calls=%async_computation.9 | async-start | bytes 1572864 | tf_op jit(solution)/shard_map/all_gather | solution.py:159
  218.2 46.0 %all-gather.12.cloned.1.call-start = ((), (), s32[]{:S(2)}) async-start(), calls=%async_computation.10 | async-start | bytes 2621440 | tf_op jit(solution)/shard_map/all_gather | solution.py:173
  231.6 352.4 %all-gather.14.cloned.1.call-start = ((), (), s32[]{:S(2)}) async-start(), calls=%async_computation.11 | async-start | bytes 22282240 | tf_op jit(solution)/shard_map/all_gather | solution.py:146
  238.2 345.8 %copy-start.13 = (f32[1,8192]{1,0:T(1,128)S(1)}, f32[1,8192]{1,0:T(1,128)}, u32[]{:S(2)}) copy-start(f32[1,8192]{1,0:T(1,128)} %param.24) | copy-start | bytes 98308
  238.2 357.2 %all-to-all-start = ((bf16[16,1,512,1024]{3,2,1,0:T(8,128)(2,1)}), bf16[16,1,512,1024]{3,2,1,0:T(8,128)(2,1)}, u32[]{:S(2)}, u32[]{:S(2)}) async-start(bf16[16,1,512,1024]{3,2,1,0:T(8,128)(2,1)} %stack.8), calls=%async_computation.1 | async-start | bytes 33554432 | tf_op jit(solution)/shard_map/all_to_all | solution.py:148
  245.3 407.8 %reduce-scatter.7.cloned.1.call-start = ((), (), s32[]{:S(2)}) async-start(), calls=%async_computation.12 | async-start | bytes 2621440 | tf_op jit(solution)/shard_map/reduce_scatter | solution.py:180
  595.4 57.7 %copy-start.4 = (bf16[256,2048]{1,0:T(8,128)(2,1)S(1)}, bf16[256,2048]{1,0:T(8,128)(2,1)}, u32[]{:S(2)}) copy-start(bf16[256,2048]{1,0:T(8,128)(2,1)} %all-gather.10.cloned.1.call-done) | copy-start | bytes 3145732
  608.3 81.0 %all-gather.16.cloned.1.call-start = ((), (), s32[]{:S(2)}) async-start(), calls=%async_computation.13 | async-start | bytes 2621440 | tf_op jit(solution)/shard_map/all_gather | solution.py:173
  654.3 3.3 collective-permute-start
  658.5 87.1 %reduce-scatter.9.cloned.1.call-start = ((), (), s32[]{:S(2)}) async-start(), calls=%async_computation.14 | async-start | bytes 2621440 | tf_op jit(solution)/shard_map/reduce_scatter | solution.py:180
  658.5 3.1 collective-permute-start.1
  702.8 42.7 %copy-start.2 = (bf16[128,2048]{1,0:T(8,128)(2,1)S(1)}, bf16[128,2048]{1,0:T(8,128)(2,1)}, u32[]{:S(2)}) copy-start(bf16[128,2048]{1,0:T(8,128)(2,1)} %slice_select_fusion.1) | copy-start | bytes 1572868
  715.6 35.3 %copy-start.9 = (bf16[128,2048]{1,0:T(8,128)(2,1)S(1)}, bf16[128,2048]{1,0:T(8,128)(2,1)}, u32[]{:S(2)}) copy-start(bf16[128,2048]{1,0:T(8,128)(2,1)} %param.27) | copy-start | bytes 1572868
  715.6 66.1 %all-gather.18.cloned.1.call-start = ((), (), s32[]{:S(2)}) async-start(), calls=%async_computation.15 | async-start | bytes 2621440 | tf_op jit(solution)/shard_map/all_gather | solution.py:173
  746.7 7.3 copy-start.5
  746.7 3.3 collective-permute-start.2
  754.0 70.8 %all-to-all-start.1 = ((bf16[16,64,2048]{2,1,0:T(8,128)(2,1)}), bf16[16,64,2048]{2,1,0:T(8,128)(2,1)}, u32[]{:S(2)}, u32[]{:S(2)}) async-start(bf16[16,64,2048]{2,1,0:T(8,128)(2,1)} %bitcast.180), calls=%async_computation.5 | async-start | bytes 8388608 | tf_op jit(solution)/shard_map/all_to_all | solution.py:195
  760.9 77.1 %reduce-scatter.11.cloned.1.call-start = ((), (), s32[]{:S(2)}) async-start(), calls=%async_computation.16 | async-start | bytes 2621440 | tf_op jit(solution)/shard_map/reduce_scatter | solution.py:180
  760.9 2.8 collective-permute-start.3
  831.3 53.5 %all-to-all-start.2 = ((bf16[16,64,2048]{2,0,1:T(8,128)(2,1)}), bf16[16,64,2048]{2,0,1:T(8,128)(2,1)}, u32[]{:S(2)}, u32[]{:S(2)}) async-start(bf16[16,64,2048]{2,0,1:T(8,128)(2,1)} %copy.122), calls=%async_computation.6 | async-start | bytes 8388608 | tf_op jit(solution)/shard_map/all_to_all | solution.py:194
  836.3 53.2 %all-reduce.3.cloned.1.call-start = ((), (), s32[]{:S(2)}) async-start(), calls=%async_computation.17 | async-start | bytes 2097152 | tf_op jit(solution)/shard_map/psum | solution.py:25
  839.2 52.2 %copy-start.1 = (bf16[1280,1280]{1,0:T(8,128)(2,1)S(1)}, bf16[1280,1280]{1,0:T(8,128)(2,1)}, u32[]{:S(2)}) copy-start(bf16[1280,1280]{1,0:T(8,128)(2,1)} %param.18) | copy-start | bytes 9830404
  (4 other events, 15.5 us)
Sparse Core Ops, SparseCore 0:
  33.0 87.8 all-gather.7
  131.8 84.4 reduce-scatter.4
  218.5 11.1 all-gather.9
  231.8 32.4 all-gather.11
  266.2 317.7 all-gather.13
  608.4 44.6 reduce-scatter.6
  658.6 30.6 all-gather.15
  715.8 29.7 reduce-scatter.8
  751.0 30.6 all-gather.17
  808.2 29.7 reduce-scatter.10
  841.7 26.6 all-reduce.2
